TPU v7x, 32 devices: a whole 2x2x4 slice. The times are simulated.
32 devices in a mesh: ctx: 8 (over z, x), head: 4 (over y, core).
Axes of the slice: x: 2, y: 2, z: 4, core: 2. Of those that a mesh axis runs over, the one named last changes fastest.
Arguments:
- queries: bfloat16 [4096, 4096], P('ctx', 'head'), may hold values from -8 to 8
- keys: bfloat16 [4096, 512], P('ctx', 'head'), may hold values from -8 to 8
- values: bfloat16 [4096, 512], P('ctx', 'head'), may hold values from -6 to 6
- distances: int32 [4, 3], P('head'), may hold values from 1 to 7, as said below
- out_weight: bfloat16 [4096, 2048], P('head'), may hold values from -0.09375 to 0.09375
- residual: bfloat16 [4096, 2048], P(('ctx', 'head')), may hold values from -6 to 6
- norm_gain: float32 [2048], replicated, may hold values from 0.25 to 1.75
- expert_gate_up: bfloat16 [32, 2048, 1536], P(('ctx', 'head')), may hold values from -0.125 to 0.125
- expert_down: bfloat16 [32, 768, 2048], P(('ctx', 'head')), may hold values from -0.21875 to 0.21875
- routes: int32 [4096, 8], P(('ctx', 'head')), may hold values from 0 to 31, all different within a row; in each aligned block of 128 rows (0 to 127, 128 to 255, ...) at most 64 rows name the same one
- route_weights: float32 [4096, 8], P(('ctx', 'head')), may hold values from 0.05 to 0.5
Outputs:
- attended: bfloat16 [4096, 2048], P(('ctx', 'head'))
- moe_out: bfloat16 [4096, 2048], P(('ctx', 'head'))
Inputs may be any that keep to these rules, and one draw needn't show every extreme that they name: Each row holds 3 different distances; some row holds the distance 4096 // 1024. `routes`: among the 128 rows of one device, no expert is named by more than 64 rows.
All inputs are finite; a program needn't handle non-finite values.
Results may differ from a plain program's by a relative error of at most 0.01.
Values may be sent and summed in bfloat16 or wider, within the bound.
A program may use at most 128 MiB of HBM per device.

v0:
```python
import math

import jax
import jax.numpy as jnp
from jax import lax
from jax.sharding import PartitionSpec as P

HD = 128
FFE = 768
TOP = 8
EXP_DEV = 1
BLK = 128
DIST = 3


def expert_rows(arrived, expert_gate_up, expert_down, sources):
    width = arrived.shape[2]
    grid = arrived.reshape(sources, EXP_DEV, arrived.shape[1], width)
    projected = jnp.einsum(
        "sekd,edf->eskf", grid, expert_gate_up, preferred_element_type=jnp.float32
    )
    hidden = (jax.nn.silu(projected[..., :FFE]) * projected[..., FFE:]).astype(jnp.bfloat16)
    output = jnp.einsum("eskf,efd->sekd", hidden, expert_down, preferred_element_type=jnp.float32)
    return output.astype(jnp.bfloat16).reshape(arrived.shape)


def body(
    queries,
    keys,
    values,
    distances,
    out_weight,
    residual,
    norm_gain,
    expert_gate_up,
    expert_down,
    routes,
    route_weights,
):
    length = queries.shape[0]
    groups = queries.shape[1] // HD
    blocks = length // BLK
    scale = 1.0 / math.sqrt(HD)
    wanted = distances[0]
    source = lax.axis_index("ctx") - wanted
    usable = source >= 0
    packed = jnp.concatenate([keys, values], axis=1)
    everything = lax.all_gather(packed, "ctx", axis=0, tiled=True)
    offsets = jnp.maximum(source, 0) * length
    fetched = jnp.stack(
        [
            lax.dynamic_slice_in_dim(everything, offsets[slot_index], length, 0)
            for slot_index in range(DIST)
        ]
    )
    query = queries.reshape(length, groups, HD)
    causal = jnp.arange(length)[:, None] >= jnp.arange(length)[None, :]
    local = jnp.einsum("tgd,ud->gtu", query, keys, preferred_element_type=jnp.float32) * scale
    local = jnp.where(causal[None], local, -jnp.inf)
    far_keys = fetched[:, :, :HD].reshape(DIST, blocks, BLK, HD)
    far_values = fetched[:, :, HD:].reshape(DIST, blocks, BLK, HD)
    query_blocks = queries.reshape(blocks, BLK, groups, HD)
    remote = (
        jnp.einsum("bqgd,jbud->gjbqu", query_blocks, far_keys, preferred_element_type=jnp.float32)
        * scale
    )
    remote = jnp.where(usable[None, :, None, None, None], remote, -jnp.inf)
    highest = jnp.maximum(local.max(-1), remote.max(axis=(1, 4)).reshape(groups, length))
    near_weight = jnp.exp(local - highest[:, :, None])
    far_weight = jnp.exp(remote - highest.reshape(groups, blocks, BLK)[:, None, :, :, None])
    denominator = near_weight.sum(-1) + far_weight.sum(axis=(1, 4)).reshape(groups, length)
    mixed = jnp.einsum(
        "gtu,ud->tgd", near_weight.astype(jnp.bfloat16), values, preferred_element_type=jnp.float32
    )
    far_mixed = jnp.einsum(
        "gjbqu,jbud->bqgd",
        far_weight.astype(jnp.bfloat16),
        far_values,
        preferred_element_type=jnp.float32,
    )
    mixed = mixed + far_mixed.reshape(length, groups, HD)
    attention = (
        (mixed / jnp.transpose(denominator)[:, :, None])
        .astype(jnp.bfloat16)
        .reshape(length, groups * HD)
    )
    summed = lax.psum_scatter(
        jnp.dot(attention, out_weight, preferred_element_type=jnp.float32),
        "head",
        scatter_dimension=0,
        tiled=True,
    )
    attended = (residual.astype(jnp.float32) + summed).astype(jnp.bfloat16)
    widened = attended.astype(jnp.float32)
    inverse = lax.rsqrt(jnp.mean(widened * widened, axis=-1, keepdims=True) + 1e-06)
    normed = (widened * inverse * norm_gain).astype(jnp.bfloat16)
    local_rows = normed.shape[0]
    width = normed.shape[1]
    devices = lax.axis_size(("ctx", "head"))
    experts = devices * EXP_DEV
    capacity = max(2, 2 * local_rows * TOP // experts)
    flat_experts = routes.reshape(local_rows * TOP)
    onehot = (flat_experts[:, None] == jnp.arange(experts, dtype=jnp.int32)[None, :]).astype(
        jnp.int32
    )
    places = jnp.sum(jnp.cumsum(onehot, axis=0) * onehot, axis=1) - 1
    owners = jnp.arange(local_rows * TOP, dtype=jnp.int32) // TOP
    outgoing = (
        jnp.zeros((experts, capacity, width), jnp.bfloat16)
        .at[flat_experts, places]
        .set(normed[owners])
    )
    answered = expert_rows(
        lax.all_to_all(outgoing, ("ctx", "head"), split_axis=0, concat_axis=0, tiled=True),
        expert_gate_up,
        expert_down,
        devices,
    )
    returned = lax.all_to_all(answered, ("ctx", "head"), split_axis=0, concat_axis=0, tiled=True)
    picked = returned[flat_experts, places].astype(jnp.float32)
    weighted = route_weights.reshape(local_rows * TOP)[:, None] * picked
    moe_out = weighted.reshape(local_rows, TOP, width).sum(axis=1).astype(jnp.bfloat16)
    return (attended, moe_out)


def solution(mesh):
    return jax.shard_map(
        body,
        mesh=mesh,
        in_specs=(
            P("ctx", "head"),
            P("ctx", "head"),
            P("ctx", "head"),
            P("head", None),
            P("head", None),
            P(("ctx", "head"), None),
            P(),
            P(("ctx", "head"), None, None),
            P(("ctx", "head"), None, None),
            P(("ctx", "head"), None),
            P(("ctx", "head"), None),
        ),
        out_specs=(P(("ctx", "head"), None), P(("ctx", "head"), None)),
        check_vma=False,
    )
```

profile of v0, /device:TPU:6, one launch (start us, length us, event | category | flops | bytes accessed | tf_op | source)
XLA Modules:
  0.0 609.7 jit_solution(3189925281521371265)
XLA Ops:
  7.2 0.0 copy-start
  7.2 0.0 all-gather.2.cloned.1.call-start
  7.2 1.9 pad_maximum_fusion.1
  9.1 0.0 all-gather.2.cloned.1.call-update
  9.1 0.0 reduce-scatter.2.cloned.1.call-start
  9.2 0.7 maximum_multiply_fusion
  9.8 0.7 fusion.47
  14.3 2.5 copy.50
  18.7 0.1 iota_compare_fusion
  18.8 0.7 compare_bitcast_fusion
  19.4 2.3 bitcast_bitcast_fusion
  21.7 6.0 fusion.3
  27.7 32.4 %all-gather.2.cloned.1.call-done = bf16[4096,256]{1,0:T(8,128)(2,1)} async-done(((bf16[512,256]{1,0:T(8,128)(2,1)}), bf16[4096,256]{1,0:T(8,128)(2,1)}) %all-gather.2.cloned.1.call-update) | async-done | bytes 2097168 | tf_op jit(solution)/shard_map/all_gather | solution.py:48
  60.1 1.3 dynamic-slice_bitcast_fusion.2
  61.4 0.1 pad_maximum_fusion
  61.5 0.1 fusion.46
  61.7 2.2 bitcast_reduce_fusion
  63.9 2.2 fusion.7
  66.1 2.5 fusion.22
  68.6 3.5 copy.27
  72.1 0.0 copy-start.4
  72.1 3.1 reshape.226
  75.2 5.3 fusion.1
  80.4 0.0 copy-done.5
  80.5 0.0 copy-done.4
  80.5 0.0 copy-done.3
  80.5 0.0 copy-start.1
  80.5 5.7 fusion.21
  86.2 0.0 copy-done.1
  86.2 0.0 copy-start.7
  86.2 0.0 copy-start.10
  86.3 0.0 copy-start.9
  86.3 4.4 fusion.48
  90.6 0.0 reduce-scatter.2.cloned.1.call-update
  90.7 0.0 copy-done.7
  90.7 0.1 copy.29
  90.8 0.1 eq.29
  90.9 0.1 eq.25
  91.0 0.1 reshape.229
  91.1 9.0 %reduce-window.6 = s32[32,8,128]{2,1,0:T(8,128)S(1)} reduce-window(s32[32,8,128]{2,1,0:T(8,128)S(1)} %fusion.41, s32[]{:T(128)} %constant.46.clone.1), window={size=1x1x128 pad=0_0x0_0x127_0}, to_apply=%region_5.6 | reduce-window | flops 4161536 | bytes 262148 | tf_op jit(solution)/shard_map/reduce-window
  100.1 0.1 slice.45
  100.2 0.1 copy.32
  100.4 0.1 copy.33
  100.5 0.1 broadcast_add_fusion
  100.7 0.0 copy-done.10
  100.7 0.1 multiply_reduce_fusion
  100.7 0.0 copy-done.9
  100.8 0.1 and_reduce_fusion
  100.9 33.1 %reduce-scatter.2.cloned.1.call-done = f32[128,2048]{1,0:T(8,128)} async-done(((f32[512,2048]{1,0:T(8,128)}), f32[128,2048]{1,0:T(8,128)}) %reduce-scatter.2.cloned.1.call-update) | async-done | bytes 1048592 | tf_op jit(solution)/shard_map/reduce_scatter | solution.py:87
  133.9 1.6 fusion.27
  135.6 0.8 copy-done.2
  136.3 0.0 copy-done.6
  136.3 1.0 fusion.29
  137.3 25.7 %scatter_custom_fusion = bf16[2048,2048]{1,0:T(8,128)(2,1)} fusion(s32[1024]{0:T(1024)S(1)} %get-tuple-element.24, bf16[128,2048]{1,0:T(8,128)(2,1)} %fusion.29, s32[1024]{0:T(1024)S(1)} %get-tuple-element.23, bf16[]{:T(256)} %constant.50.clone.1), kind=kCustom, calls=%fused_computation.21 | custom fusion | bytes 8389120
  163.0 189.3 %all_to_all.10 = bf16[32,64,2048]{2,1,0:T(8,128)(2,1)S(1)} all-to-all(bf16[32,64,2048]{2,1,0:T(8,128)(2,1)} %bitcast.124), channel_id=1, replica_groups=mesh['ctx'=8,'head'=4] {'ctx','head'}, dimensions={0} | all-to-all | bytes 16777216 | tf_op jit(solution)/shard_map/all_to_all | solution.py:114
  352.3 15.6 %convolution_bitcast_fusion = f32[1,32,64,1536]{3,2,1,0:T(8,128)S(1)} fusion(bf16[32,64,2048]{2,1,0:T(8,128)(2,1)S(1)} %all_to_all.10, bf16[1,2048,1536]{2,1,0:T(8,128)(2,1)} %param.18), kind=kOutput, calls=%fused_computation.9 | convolution fusion | flops 12884901888 | bytes 27262976 | tf_op jit(solution)/shard_map/sekd,edf->eskf/dot_general | solution.py:19
  367.9 0.0 copy-done
  367.9 8.9 %convolution_convert_fusion = bf16[32,64,2048]{2,1,0:T(8,128)(2,1)} fusion(bf16[1,768,2048]{2,1,0:T(8,128)(2,1)S(1)} %copy-done, f32[1,32,64,1536]{3,2,1,0:T(8,128)S(1)} %convolution_bitcast_fusion), kind=kOutput, calls=%fused_computation.18 | convolution fusion | flops 6456082432 | bytes 24117248 | tf_op jit(solution)/shard_map/eskf,efd->sekd/dot_general | solution.py:23
  376.9 4.5 all-to-all-start.1
  381.4 0.0 copy-done.8
  381.4 0.1 copy.28
  381.5 188.2 %all-to-all-done.1 = bf16[32,64,2048]{2,1,0:T(8,128)(2,1)} async-done(((bf16[32,64,2048]{2,1,0:T(8,128)(2,1)}), bf16[32,64,2048]{2,1,0:T(8,128)(2,1)}, u32[]{:S(2)}, u32[]{:S(2)}) %all-to-all-start.1) | async-done | bytes 8388640 | tf_op jit(solution)/shard_map/all_to_all | solution.py:119
  569.7 25.6 %gather_fusion = bf16[1024,2048]{1,0:T(8,128)(2,1)} fusion(bf16[32,64,2048]{2,1,0:T(8,128)(2,1)} %all-to-all-done.1, s32[1024]{0:T(1024)S(1)} %bitcast.123), kind=kCustom, calls=%fused_computation.1 | custom fusion | bytes 8396800 | tf_op jit(solution)/shard_map/gather | solution.py:120
  595.2 7.3 %fusion = bf16[128,2048]{1,0:T(8,128)(2,1)} fusion(bf16[1024,2048]{1,0:T(8,128)(2,1)} %gather_fusion, f32[128,8]{1,0:T(8,128)S(1)} %copy.28), kind=kLoop, calls=%fused_computation.4 | loop fusion | flops 6029312 | bytes 4722688 | tf_op jit(solution)/shard_map/reduce_sum | solution.py:122
  (17 shorter events, 0.2 us)
Async XLA Ops:
  7.2 360.8 %copy-start = (bf16[1,768,2048]{2,1,0:T(8,128)(2,1)S(1)}, bf16[1,768,2048]{2,1,0:T(8,128)(2,1)}, u32[]{:S(2)}) copy-start(bf16[1,768,2048]{2,1,0:T(8,128)(2,1)} %param.19) | copy-start | bytes 9437188
  7.2 52.9 %all-gather.2.cloned.1.call-start = ((), (), s32[]{:S(2)}) async-start(), calls=%async_computation.3 | async-start | bytes 2359296 | tf_op jit(solution)/shard_map/all_gather | solution.py:48
  9.1 124.8 %reduce-scatter.2.cloned.1.call-start = ((), (), s32[]{:S(2)}) async-start(), calls=%async_computation.4 | async-start | bytes 5242880 | tf_op jit(solution)/shard_map/reduce_scatter | solution.py:87
  72.1 8.4 %copy-start.4 = (bf16[512,128]{1,0:T(8,128)(2,1)S(1)}, bf16[512,128]{1,0:T(8,128)(2,1)}, u32[]{:S(2)}) copy-start(bf16[512,128]{1,0:T(8,128)(2,1)} %param.13) | copy-start | bytes 393220
  75.2 5.3 copy-start.5
  75.2 5.3 copy-start.3
  80.5 5.7 copy-start.1
  86.2 4.4 copy-start.7
  86.2 14.4 %copy-start.10 = (s32[2]{0:T(128)S(1)}, s32[2]{0:T(128)}, u32[]{:S(2)}) copy-start(s32[2]{0:T(128)} %constant.64) | copy-start | bytes 28
  86.3 14.5 %copy-start.9 = (s32[2]{0:T(128)S(1)}, s32[2]{0:T(128)}, u32[]{:S(2)}) copy-start(s32[2]{0:T(128)} %constant.67) | copy-start | bytes 28
  90.6 45.7 %copy-start.6 = (f32[2048]{0:T(1024)S(1)}, f32[2048]{0:T(1024)}, u32[]{:S(2)}) copy-start(f32[2048]{0:T(1024)} %param.17) | copy-start | bytes 24580
  135.5 0.8 copy-start.2
  376.9 4.5 copy-start.8
  376.9 192.8 %all-to-all-start.1 = ((bf16[32,64,2048]{2,1,0:T(8,128)(2,1)}), bf16[32,64,2048]{2,1,0:T(8,128)(2,1)}, u32[]{:S(2)}, u32[]{:S(2)}) async-start(bf16[32,64,2048]{2,1,0:T(8,128)(2,1)} %convolution_convert_fusion), calls=%async_computation.2 | async-start | bytes 16777216 | tf_op jit(solution)/shard_map/all_to_all | solution.py:119
Sparse Core Ops, SparseCore 0:
  10.7 49.3 all-gather.1
  90.8 43.1 reduce-scatter.1
where the time goes:
time: 616 us; the launch traced here: 610 us
  waiting for transfers between devices  254 us (41%)
  blocking collectives  189 us (31%)
  local copies, waits for them, and re-layouts  66.4 us (11%)
  matrix products  45.3 us (7%)
  other arithmetic  30.2 us (5%)
  between operations  20.3 us (3%)
    all_to_all x1, blocking collectives, body(): lax.all_to_all(outgoing, ('ctx', 'head'), split_axis=0, concat_axis=0, ti...  189 us
    all_to_all x1, waiting for transfers between devices, body(): lax.all_to_all(answered, ('ctx', 'head'), split_axis=0, concat_axis=0, ti...  188 us
    reduce_scatter x1, waiting for transfers between devices, body(): lax.psum_scatter(jnp.dot(attention, out_weight, preferred_element_type=jn...  33.1 us
    all_gather x1, waiting for transfers between devices, body(): everything = lax.all_gather(packed, 'ctx', axis=0, tiled=True)  32.4 us
    unnamed x26, local copies, waits for them, and re-layouts  29.2 us
    gather x1, local copies, waits for them, and re-layouts, body(): picked = returned[flat_experts, places].astype(jnp.float32)  25.6 us
    dot_general x1, matrix products, expert_rows(): jnp.einsum('sekd,edf->eskf', grid, expert_gate_up, preferred_element_type...  15.6 us
  transfers between devices with their start and end apart: 3, of which 3 were waited for; matrix products, arithmetic and copies ran while one was open for 4% of the time, Pallas kernels for 0%

commit v1 on v0

--- a/solution.py
+++ b/solution.py
@@ -24,6 +24,65 @@
     return output.astype(jnp.bfloat16).reshape(arrived.shape)
 
 
+def routed_experts(normed, expert_gate_up, expert_down, routes, route_weights, capacity):
+    local_rows, width = normed.shape
+    devices = lax.axis_size(("ctx", "head"))
+    experts = devices * EXP_DEV
+    flat_experts = routes.reshape(local_rows * TOP)
+    onehot = (flat_experts[:, None] == jnp.arange(experts, dtype=jnp.int32)[None, :]).astype(
+        jnp.int32
+    )
+    places = jnp.sum(jnp.cumsum(onehot, axis=0) * onehot, axis=1) - 1
+    owners = jnp.arange(local_rows * TOP, dtype=jnp.int32) // TOP
+    outgoing = (
+        jnp.zeros((experts, capacity, width), jnp.bfloat16)
+        .at[flat_experts, places]
+        .set(normed[owners])
+    )
+    answered = expert_rows(
+        lax.all_to_all(outgoing, ("ctx", "head"), split_axis=0, concat_axis=0, tiled=True),
+        expert_gate_up,
+        expert_down,
+        devices,
+    )
+    returned = lax.all_to_all(answered, ("ctx", "head"), split_axis=0, concat_axis=0, tiled=True)
+    picked = returned[flat_experts, places].astype(jnp.float32)
+    weighted = route_weights.reshape(local_rows * TOP)[:, None] * picked
+    moe_out = weighted.reshape(local_rows, TOP, width).sum(axis=1).astype(jnp.bfloat16)
+    return moe_out
+
+
+def dense_experts(normed, expert_gate_up, expert_down, table, capacity):
+    local_rows, width = normed.shape
+    axes = ("ctx", "head")
+    sources = table.shape[0]
+    mine = lax.axis_index(axes).astype(jnp.float32)
+    chosen = table[:, :, :TOP] == mine
+    weight = jnp.sum(jnp.where(chosen, table[:, :, TOP:], 0.0), axis=2)
+    named = jnp.any(chosen, axis=2)
+    earlier = jnp.arange(local_rows)[:, None] < jnp.arange(local_rows)[None, :]
+    places = jnp.dot(
+        named.astype(jnp.bfloat16), earlier.astype(jnp.bfloat16), preferred_element_type=jnp.float32
+    ).astype(jnp.int32)
+    select = (
+        named[:, None, :] & (places[:, None, :] == jnp.arange(capacity, dtype=jnp.int32)[None, :, None])
+    ).astype(jnp.bfloat16)
+    everyone = lax.all_gather(normed, axes, axis=0, tiled=False)
+    rows = jnp.einsum(
+        "sct,std->scd", select, everyone, preferred_element_type=jnp.float32
+    ).astype(jnp.bfloat16)
+    rows = rows.reshape(sources * capacity, width)
+    projected = jnp.dot(rows, expert_gate_up[0], preferred_element_type=jnp.float32)
+    hidden = (jax.nn.silu(projected[:, :FFE]) * projected[:, FFE:]).astype(jnp.bfloat16)
+    output = jnp.dot(hidden, expert_down[0], preferred_element_type=jnp.float32).astype(jnp.bfloat16)
+    output = output.reshape(sources, capacity, width)
+    spread = jnp.einsum("sct,scd->std", select, output, preferred_element_type=jnp.float32)
+    partial = (weight[:, :, None] * spread).astype(jnp.bfloat16)
+    return lax.psum_scatter(
+        partial.reshape(sources * local_rows, width), axes, scatter_dimension=0, tiled=True
+    )
+
+
 def body(
     queries,
     keys,
@@ -41,6 +100,12 @@
     groups = queries.shape[1] // HD
     blocks = length // BLK
     scale = 1.0 / math.sqrt(HD)
+    table = lax.all_gather(
+        jnp.concatenate([routes.astype(jnp.float32), route_weights], axis=1),
+        ("ctx", "head"),
+        axis=0,
+        tiled=False,
+    )
     wanted = distances[0]
     source = lax.axis_index("ctx") - wanted
     usable = source >= 0
@@ -85,12 +150,12 @@
         .reshape(length, groups * HD)
     )
     summed = lax.psum_scatter(
-        jnp.dot(attention, out_weight, preferred_element_type=jnp.float32),
+        jnp.dot(attention, out_weight, preferred_element_type=jnp.float32).astype(jnp.bfloat16),
         "head",
         scatter_dimension=0,
         tiled=True,
     )
-    attended = (residual.astype(jnp.float32) + summed).astype(jnp.bfloat16)
+    attended = (residual.astype(jnp.float32) + summed.astype(jnp.float32)).astype(jnp.bfloat16)
     widened = attended.astype(jnp.float32)
     inverse = lax.rsqrt(jnp.mean(widened * widened, axis=-1, keepdims=True) + 1e-06)
     normed = (widened * inverse * norm_gain).astype(jnp.bfloat16)
@@ -99,27 +164,14 @@
     devices = lax.axis_size(("ctx", "head"))
     experts = devices * EXP_DEV
     capacity = max(2, 2 * local_rows * TOP // experts)
-    flat_experts = routes.reshape(local_rows * TOP)
-    onehot = (flat_experts[:, None] == jnp.arange(experts, dtype=jnp.int32)[None, :]).astype(
-        jnp.int32
-    )
-    places = jnp.sum(jnp.cumsum(onehot, axis=0) * onehot, axis=1) - 1
-    owners = jnp.arange(local_rows * TOP, dtype=jnp.int32) // TOP
-    outgoing = (
-        jnp.zeros((experts, capacity, width), jnp.bfloat16)
-        .at[flat_experts, places]
-        .set(normed[owners])
-    )
-    answered = expert_rows(
-        lax.all_to_all(outgoing, ("ctx", "head"), split_axis=0, concat_axis=0, tiled=True),
-        expert_gate_up,
-        expert_down,
-        devices,
-    )
-    returned = lax.all_to_all(answered, ("ctx", "head"), split_axis=0, concat_axis=0, tiled=True)
-    picked = returned[flat_experts, places].astype(jnp.float32)
-    weighted = route_weights.reshape(local_rows * TOP)[:, None] * picked
-    moe_out = weighted.reshape(local_rows, TOP, width).sum(axis=1).astype(jnp.bfloat16)
+    if devices * local_rows <= 2 * experts * capacity:
+        moe_out = dense_experts(
+            normed, expert_gate_up, expert_down, table, capacity
+        )
+    else:
+        moe_out = routed_experts(
+            normed, expert_gate_up, expert_down, routes, route_weights, capacity
+        )
     return (attended, moe_out)
 
 

time: 616 us -> 478 us (0.78)
  blocking collectives: 189 us -> 35.9 us
  waiting for transfers between devices: 254 us -> 325 us
  local copies, waits for them, and re-layouts: 66.4 us -> 13.9 us
  matrix products: 45.3 us -> 68.3 us
  other arithmetic: 30.2 us -> 13.4 us
    all_to_all x1 -> x0, blocking collectives: 189 us -> none  [body(): lax.all_to_all(outgoing, ('ctx', 'head'), split_axis=0, concat_axis=0, ti...]
    all_to_all x1 -> x0, waiting for transfers between devices: 188 us -> none  [body(): lax.all_to_all(answered, ('ctx', 'head'), split_axis=0, concat_axis=0, ti...]
    reduce_scatter x0 -> x1, waiting for transfers between devices: none -> 184 us  [dense_experts(): lax.psum_scatter(partial.reshape(sources * local_rows, width), axes, scat...]
    all_gather x0 -> x1, waiting for transfers between devices: none -> 78.9 us  [dense_experts(): everyone = lax.all_gather(normed, axes, axis=0, tiled=False)]
    all_gather x0 -> x1, blocking collectives: none -> 35.9 us  [body(): lax.all_gather(jnp.concatenate([routes.astype(jnp.float32), route_weights...]
    unnamed x26 -> x20, local copies, waits for them, and re-layouts: 29.2 us -> 3.35 us
    gather x1 -> x0, local copies, waits for them, and re-layouts: 25.6 us -> none  [body(): picked = returned[flat_experts, places].astype(jnp.float32)]
    dot_general x2 -> x5, matrix products: 24.6 us -> 48.1 us  [the longest x1 17.4 us: dense_experts(): jnp.dot(rows, expert_gate_up[0], preferred_element_type=jnp.float32)]
  transfers between devices with their start and end apart: 3 -> 4, of which waited for: 3 -> 4; matrix products, arithmetic and copies ran while one was open for 4% -> 3% of each run, Pallas kernels for 0% -> 0%
where the time goes in v1:
time: 478 us; the launch traced here: 476 us
  waiting for transfers between devices  325 us (68%)
  matrix products  68.3 us (14%)
  blocking collectives  35.9 us (8%)
  between operations  19.6 us (4%)
  local copies, waits for them, and re-layouts  13.9 us (3%)
  other arithmetic  13.4 us (3%)
    reduce_scatter x1, waiting for transfers between devices, dense_experts(): lax.psum_scatter(partial.reshape(sources * local_rows, width), axes, scat...  184 us
    all_gather x1, waiting for transfers between devices, dense_experts(): everyone = lax.all_gather(normed, axes, axis=0, tiled=False)  78.9 us
    all_gather x1, blocking collectives, body(): lax.all_gather(jnp.concatenate([routes.astype(jnp.float32), route_weights...  35.9 us
    all_gather x1, waiting for transfers between devices, body(): everything = lax.all_gather(packed, 'ctx', axis=0, tiled=True)  32.5 us
    reduce_scatter x1, waiting for transfers between devices, body(): lax.psum_scatter(jnp.dot(attention, out_weight, preferred_element_type=jn...  29.7 us
    dot_general x1, matrix products, dense_experts(): jnp.dot(rows, expert_gate_up[0], preferred_element_type=jnp.float32)  17.4 us
    dot_general x1, matrix products, dense_experts(): jnp.einsum('sct,std->scd', select, everyone, preferred_element_type=jnp.f...  11.3 us
    dot_general x1, matrix products, dense_experts(): jnp.einsum('sct,scd->std', select, output, preferred_element_type=jnp.flo...  10.3 us
  transfers between devices with their start and end apart: 4, of which 4 were waited for; matrix products, arithmetic and copies ran while one was open for 3% of the time, Pallas kernels for 0%

profile of v1, /device:TPU:6, one launch (start us, length us, event | category | flops | bytes accessed | tf_op | source)
XLA Modules:
  0.0 476.0 jit_solution(13756306924504071667)
XLA Ops:
  7.2 0.0 copy-start
  7.2 0.0 all-gather.5.cloned.1.call-start
  7.2 1.9 pad_maximum_fusion.1
  9.1 0.0 all-gather.5.cloned.1.call-update
  9.1 0.0 reduce-scatter.3.cloned.1.call-start
  9.2 0.7 maximum_multiply_fusion
  9.8 0.6 fusion.50
  14.2 2.5 copy.43
  18.5 0.1 iota_compare_fusion.1
  18.6 0.7 compare_bitcast_fusion
  19.3 2.3 bitcast_bitcast_fusion
  21.6 6.0 %fusion.2 = (f32[8,512]{1,0:T(8,128)S(1)}, f32[512,512,8]{1,0,2:T(8,128)}) fusion(pred[512,512]{0,1:T(8,128)(4,1)S(1)} %iota_compare_fusion.1, bf16[512,128]{1,0:T(8,128)(2,1)} %param.12, bf16[512,1024]{1,0:T(8,128)(2,1)} %param.11), kind=kOutput, calls=%fused_computation.6 | convolution fusion | flops 543158272 | bytes 9846784 | tf_op jit(solution)/shard_map/tgd,ud->gtu/dot_general | solution.py:123
  27.5 32.5 %all-gather.5.cloned.1.call-done = bf16[4096,256]{1,0:T(8,128)(2,1)} async-done(((bf16[512,256]{1,0:T(8,128)(2,1)}), bf16[4096,256]{1,0:T(8,128)(2,1)}) %all-gather.5.cloned.1.call-update) | async-done | bytes 2097168 | tf_op jit(solution)/shard_map/all_gather | solution.py:113
  60.1 1.4 dynamic-slice_bitcast_fusion.2
  61.5 0.1 pad_maximum_fusion
  61.6 0.1 fusion.49
  61.7 2.2 bitcast_reduce_fusion
  64.0 2.2 fusion.7
  66.2 2.5 fusion.19
  68.7 2.9 copy.26
  71.6 0.0 copy-start.3
  71.6 3.1 reshape.101
  74.7 0.0 copy-start.4
  74.7 0.0 copy-start.1
  74.7 5.3 %fusion = f32[8,512]{1,0:T(8,128)S(1)} fusion(f32[512,512,8]{1,0,2:T(8,128)} %get-tuple-element.19, f32[8,512]{1,0:T(8,128)S(1)} %bitcast_maximum_fusion.1, pred[512,512]{0,1:T(8,128)(4,1)S(1)} %iota_compare_fusion.1), kind=kLoop, calls=%fused_computation.4 | loop fusion | flops 8384512 | bytes 8683520 | tf_op jit(solution)/shard_map/reduce_sum | solution.py:136
  80.0 0.0 copy-done.4
  80.0 0.0 copy-done.3
  80.0 0.0 copy-done.1
  80.0 0.0 copy-start.8
  80.0 5.7 %fusion.18 = bf16[512,8,128]{0,2,1:T(8,128)(2,1)S(1)} fusion(f32[512,8,128]{0,2,1:T(8,128)S(1)} %copy-done.1, f32[512,512,8]{1,0,2:T(8,128)} %get-tuple-element.19, f32[8,512]{1,0:T(8,128)S(1)} %bitcast_maximum_fusion.1, pred[512,512]{0,1:T(8,128)(4,1)S(1)} %iota_compare_fusion.1, f32[512,8]{0,1:T(8,128)S(1)} %fusion.44, bf16[512,128]{1,0:T(8,128)(2,1)S(1)} %copy-done.3), kind=kOutput, calls=%fused_computation.27 | convolution fusion | flops 546832384 | bytes 11960320 | tf_op jit(solution)/shard_map/gtu,ud->tgd/dot_general | solution.py:137
  85.7 0.0 copy-done.8
  85.7 0.0 copy-start.5
  85.8 0.0 copy-start.6
  85.8 0.0 copy-start.7
  85.8 3.8 convolution_convert_fusion.2
  89.6 0.0 reduce-scatter.3.cloned.1.call-update
  89.6 0.0 all-gather.7.cloned.1.call-start
  89.6 29.7 %reduce-scatter.3.cloned.1.call-done = bf16[128,2048]{1,0:T(8,128)(2,1)} async-done(((bf16[512,2048]{1,0:T(8,128)(2,1)}), bf16[128,2048]{1,0:T(8,128)(2,1)}) %reduce-scatter.3.cloned.1.call-update) | async-done | bytes 524304 | tf_op jit(solution)/shard_map/reduce_scatter | solution.py:152
  119.3 1.5 fusion.24
  120.8 0.0 copy-start.2
  120.8 0.8 copy-done.2
  121.6 0.0 copy-done.5
  121.6 1.0 fusion.26
  122.6 0.0 all-gather.7.cloned.1.call-update
  122.6 0.0 reduce-scatter.5.cloned.1.call-start
  122.7 0.0 copy-done.6
  122.7 0.0 copy-done.7
  122.7 35.9 %all-gather = f32[4096,16]{0,1:T(8,128)S(1)} all-gather(f32[128,16]{0,1:T(8,128)S(1)} %pad_maximum_fusion.2), channel_id=2, replica_groups=mesh['ctx'=8,'head'=4] {'ctx','head'}, dimensions={0}, use_global_device_ids=true | all-gather | bytes 270336 | tf_op jit(solution)/shard_map/all_gather | solution.py:103
  158.6 0.1 copy.44
  158.7 0.1 convolution_convert_fusion.3
  158.9 78.9 %all-gather.7.cloned.1.call-done = bf16[4096,2048]{1,0:T(8,128)(2,1)} async-done(((bf16[128,2048]{1,0:T(8,128)(2,1)}), bf16[4096,2048]{1,0:T(8,128)(2,1)}) %all-gather.7.cloned.1.call-update) | async-done | bytes 16777232 | tf_op jit(solution)/shard_map/all_gather | solution.py:70
  237.8 11.3 %convolution_convert_fusion.1 = bf16[32,64,2048]{2,1,0:T(8,128)(2,1)} fusion(bf16[32,128,2048]{2,1,0:T(8,128)(2,1)} %bitcast.106, s32[32,128]{1,0:T(8,128)S(1)} %convolution_convert_fusion.3, pred[32,128]{1,0:T(8,128)(4,1)S(1)} %get-tuple-element.2), kind=kOutput, calls=%fused_computation.15 | convolution fusion | flops 1078460416 | bytes 25186304 | tf_op jit(solution)/shard_map/sct,std->scd/dot_general | solution.py:71
  249.1 17.4 %fusion.4 = f32[2048,1536]{1,0:T(8,128)S(1)} fusion(bf16[2048,2048]{1,0:T(8,128)(2,1)} %bitcast.107, bf16[1,2048,1536]{2,1,0:T(8,128)(2,1)} %param.18), kind=kOutput, calls=%fused_computation.9 | convolution fusion | flops 12884901888 | bytes 27262976 | tf_op jit(solution)/shard_map/dot_general | solution.py:75
  266.5 0.0 copy-done
  266.5 9.0 %convolution_convert_fusion = bf16[2048,2048]{1,0:T(8,128)(2,1)} fusion(f32[2048,1536]{1,0:T(8,128)S(1)} %fusion.4, bf16[1,768,2048]{2,1,0:T(8,128)(2,1)S(1)} %copy-done), kind=kOutput, calls=%fused_computation.3 | convolution fusion | flops 6456082432 | bytes 24117248 | tf_op jit(solution)/shard_map/dot_general | solution.py:77
  275.4 10.3 %multiply_convert_fusion = bf16[32,128,2048]{2,1,0:T(8,128)(2,1)} fusion(f32[32,128]{1,0:T(8,128)S(1)} %fusion.41, bf16[32,64,2048]{2,1,0:T(8,128)(2,1)} %bitcast.108, s32[32,128]{1,0:T(8,128)S(1)} %convolution_convert_fusion.3, pred[32,128]{1,0:T(8,128)(4,1)S(1)} %get-tuple-element.2), kind=kOutput, calls=%fused_computation | convolution fusion | flops 1091043328 | bytes 25202688 | tf_op jit(solution)/shard_map/sct,scd->std/dot_general | solution.py:79
  285.8 0.0 reduce-scatter.5.cloned.1.call-update
  285.8 183.7 %reduce-scatter.5.cloned.1.call-done = bf16[128,2048]{1,0:T(8,128)(2,1)} async-done(((bf16[4096,2048]{1,0:T(8,128)(2,1)}), bf16[128,2048]{1,0:T(8,128)(2,1)}) %reduce-scatter.5.cloned.1.call-update) | async-done | bytes 524304 | tf_op jit(solution)/shard_map/reduce_scatter | solution.py:81
  (8 shorter events, 0.1 us)
Async XLA Ops:
  7.2 259.3 %copy-start = (bf16[1,768,2048]{2,1,0:T(8,128)(2,1)S(1)}, bf16[1,768,2048]{2,1,0:T(8,128)(2,1)}, u32[]{:S(2)}) copy-start(bf16[1,768,2048]{2,1,0:T(8,128)(2,1)} %param.19) | copy-start | bytes 9437188
  7.2 52.9 %all-gather.5.cloned.1.call-start = ((), (), s32[]{:S(2)}) async-start(), calls=%async_computation.2 | async-start | bytes 2359296 | tf_op jit(solution)/shard_map/all_gather | solution.py:113
  9.1 110.2 %reduce-scatter.3.cloned.1.call-start = ((), (), s32[]{:S(2)}) async-start(), calls=%async_computation.3 | async-start | bytes 2621440 | tf_op jit(solution)/shard_map/reduce_scatter | solution.py:152
  71.6 8.4 %copy-start.3 = (bf16[512,128]{1,0:T(8,128)(2,1)S(1)}, bf16[512,128]{1,0:T(8,128)(2,1)}, u32[]{:S(2)}) copy-start(bf16[512,128]{1,0:T(8,128)(2,1)} %param.13) | copy-start | bytes 393220
  74.7 5.3 %copy-start.4 = (f32[8,4,128]{2,0,1:T(8,128)S(1)}, f32[8,4,128]{2,0,1:T(8,128)}, u32[]{:S(2)}) copy-start(f32[8,4,128]{2,0,1:T(8,128)} %get-tuple-element.6) | copy-start | bytes 49156
  74.7 5.3 %copy-start.1 = (f32[512,8,128]{0,2,1:T(8,128)S(1)}, f32[512,8,128]{0,2,1:T(8,128)}, u32[]{:S(2)}) copy-start(f32[512,8,128]{0,2,1:T(8,128)} %reshape.101) | copy-start | bytes 6291460
  80.0 5.7 %copy-start.8 = (bf16[1024,2048]{1,0:T(8,128)(2,1)S(1)}, bf16[1024,2048]{1,0:T(8,128)(2,1)}, u32[]{:S(2)}) copy-start(bf16[1024,2048]{1,0:T(8,128)(2,1)} %param.15) | copy-start | bytes 12582916
  85.7 35.8 %copy-start.5 = (f32[2048]{0:T(1024)S(1)}, f32[2048]{0:T(1024)}, u32[]{:S(2)}) copy-start(f32[2048]{0:T(1024)} %param.17) | copy-start | bytes 24580
  85.8 36.9 %copy-start.6 = (s32[128,8]{0,1:T(8,128)S(1)}, s32[128,8]{0,1:T(8,128)}, u32[]{:S(2)}) copy-start(s32[128,8]{0,1:T(8,128)} %param.20) | copy-start | bytes 12292
  85.8 36.9 %copy-start.7 = (f32[128,8]{0,1:T(8,128)S(1)}, f32[128,8]{0,1:T(8,128)}, u32[]{:S(2)}) copy-start(f32[128,8]{0,1:T(8,128)} %param.21) | copy-start | bytes 12292
  89.6 148.2 %all-gather.7.cloned.1.call-start = ((), (), s32[]{:S(2)}) async-start(), calls=%async_computation.5 | async-start | bytes 17301504 | tf_op jit(solution)/shard_map/all_gather | solution.py:70
  120.8 0.8 copy-start.2
  122.6 346.9 %reduce-scatter.5.cloned.1.call-start = ((), (), s32[]{:S(2)}) async-start(), calls=%async_computation.4 | async-start | bytes 17301504 | tf_op jit(solution)/shard_map/reduce_scatter | solution.py:81
Sparse Core Ops, SparseCore 0:
  10.7 49.3 all-gather.4
  89.7 29.5 reduce-scatter.2
  122.8 114.9 all-gather.6
  285.9 183.5 reduce-scatter.4
